TPU v7x, 256 devices: a whole 4x4x8 slice. The times are simulated.
256 devices in a mesh: col: 128 (over x, y_hi, z, core), band: 2 (over y_lo).
Axes of the slice: x: 4, y: 4 (y_hi: 2, y_lo: 2; y = y_hi * 2 + y_lo), z: 8, core: 2. Of those that a mesh axis runs over, the one named last changes fastest.
Arguments:
- boundary: bfloat16 [128, 3, 128, 16, 128], P('col'), may hold values from -6 to 6
- row_tensor: bfloat16 [2, 128, 16, 16, 16, 16], P('band', 'col'), may hold values from -1.5 to 1.5
- right_proj: bfloat16 [2, 128, 3, 128, 16, 128], P('band', 'col'), may hold values from -0.125 to 0.125
- left_proj: bfloat16 [2, 128, 3, 128, 16, 128], P('band', 'col'), may hold values from -0.125 to 0.125
- kept: int32 [2, 128, 3], P('band', 'col'), may hold values from 64 to 128, as said below
Outputs:
- evolved: bfloat16 [2, 128, 3, 128, 16, 128], P('band', 'col')
Inputs may be any that keep to these rules, and one draw needn't show every extreme that they name: kept[r, c, s] counts the live states of sector s on the bond between columns c and (c + 1) mod 128; the value 128 occurs in every draw.
All inputs are finite; a program needn't handle non-finite values.
Results may differ from a plain program's by a relative error of at most 0.0095.
Values may be sent and summed in bfloat16 or wider, within the bound.
No kernel may reach another device: no remote copies, remote signals or barrier semaphores. Data moves between devices by JAX's collectives and lax.ppermute only.
A program may use at most 64 MiB of HBM per device.

v0:
```python
import functools

import jax
import jax.numpy as jnp
from jax import lax
from jax.experimental import pallas as pl
from jax.experimental.pallas import tpu as pltpu
from jax.sharding import PartitionSpec as P

F32, BF16 = jnp.float32, jnp.bfloat16
ANY = pl.BlockSpec(memory_space=pl.ANY)
HBM = pl.BlockSpec(memory_space=pltpu.HBM)
SMEM = pl.BlockSpec(memory_space=pltpu.SMEM)
VMEM = pl.BlockSpec(memory_space=pltpu.VMEM)
PARAMS = pltpu.CompilerParams(vmem_limit_bytes=28 << 20)


X, Y_HI, Z, CORES, BANDS = 4, 2, 8, 2, 2
COLS = X * Y_HI * Z * CORES


def place(column, band):
    return column * BANDS + band


def straight():
    return [(place((c - 1) % COLS, b), place(c, b)) for c in range(COLS) for b in range(BANDS)]


def around():
    first, second = [], []
    for c in range(COLS):
        for b in range(BANDS):
            here, there = place(c, b), place((c + 1) % COLS, b)
            if (c + 1) % (Z * CORES):
                first.append((here, there))
                second.append((there, there))
            else:
                x, y_hi = divmod(c // (Z * CORES), Y_HI)
                y = (y_hi * BANDS + b - 1) % (Y_HI * BANDS)
                via = place((x * Y_HI + y // BANDS) * Z * CORES, y % BANDS)
                first.append((here, via))
                second.append((via, there))
    return first, second


def in_vmem(array):
    return pltpu.with_memory_space_constraint(array, pltpu.VMEM)


def in_hbm(array):
    return pltpu.with_memory_space_constraint(array, pltpu.HBM)


def flip_right(rp, rp32, rpt):
    W, D, _ = rp.shape
    rp32[...] = rp[...].reshape(W * D, W).astype(F32)
    for t in range(D):
        rpt[t // 2, :, (t % 2) * W : (t % 2 + 1) * W] = rp32[pl.ds(t, W, stride=D), :].astype(BF16)


def contract_right(x, rpt, h):
    n, D, W = x.shape
    rows = x[...].reshape(n * D, W)
    for t in range(0, D, 2):
        y = jnp.dot(rows, rpt[t // 2], preferred_element_type=F32).astype(BF16)
        h[t] = y[:, :W].reshape(n, D, W)
        h[t + 1] = y[:, W:].reshape(n, D, W)


def contract_layer(r, h, w, at=0, n=None, unroll=32):
    D, W = h.shape[0], h.shape[-1]
    n = h.shape[1] if n is None else n
    layer = r[...]

    def step(i, _):
        a = at + 2 * i
        pair = [h[:, a + k].reshape(D * D, W) for k in range(2)]
        y = jnp.dot(layer, jnp.concatenate(pair, axis=1), preferred_element_type=F32).astype(BF16)
        for k in range(2):
            w[:, a + k] = y[:, k * W : (k + 1) * W].reshape(D, D, W)
        return 0

    lax.fori_loop(0, n // 2, step, 0, unroll=unroll)


def flip_left(lp, lpt):
    D, W = lp.shape[1:]
    lpt[...] = lp[:W].reshape(W * D, W).T


def live_mask(lp, keep_right):
    W = lp.shape[-1]
    keep_left = lp[W, 0:1, :].astype(F32)
    rows = lax.broadcasted_iota(jnp.int32, (W, W), 0).astype(F32)
    lanes = lax.broadcasted_iota(jnp.int32, (W, W), 1)
    return (rows < keep_left) & (lanes < keep_right)


def contract_left(lpt, w, acc, at=0, n=None, carried=None, live=None):
    D, W = w.shape[0], w.shape[-1]
    n = w.shape[1] if n is None else n
    left = lpt[:, at * D : (at + n) * D]
    for q in range(0, D, 2):
        pair = [w[q + k, at : at + n].reshape(n * D, W) for k in range(2)]
        y = jnp.dot(left, jnp.concatenate(pair, axis=1), preferred_element_type=F32)
        for k in range(2):
            rows = pl.ds(q + k, W, stride=D)
            z = y[:, k * W : (k + 1) * W]
            if carried is not None:
                z = z + carried[rows, :]
            if live is not None:
                z = jnp.where(live, z, 0.0)
            acc[rows, :] = z


def store(acc, outs):
    at = 0
    for out in outs:
        n, D, W = out.shape
        out[...] = acc[at * D : (at + n) * D, :].astype(BF16).reshape(out.shape)
        at += n


def spread_layer(raw, r32, r):
    D = raw.shape[0]
    rows = lax.broadcasted_iota(jnp.int32, (D, D * D), 0)
    lanes = lax.broadcasted_iota(jnp.int32, (D, D * D), 1)
    total = jnp.zeros((D * D, D * D), F32)
    for p in range(D):
        place = (lanes == rows * D + p).astype(BF16)
        total += jnp.dot(raw[:, p].reshape(D * D, D), place, preferred_element_type=F32)
    n, W = D * D, r32.shape[1]
    for i in range(n // W):
        r32[i * n : (i + 1) * n, :] = total[:, i * W : (i + 1) * W]
        for q in range(D):
            r[q * D : (q + 1) * D, i * W : (i + 1) * W] = r32[pl.ds(i * n + q, D, stride=D), :].astype(BF16)


def load(src, dst, sem):
    copy = pltpu.make_async_copy(src, dst, sem)
    copy.start()
    return copy


def send_block(s, left_proj, out, sem):
    return load(left_proj.at[0, 0, s], out.at[pl.ds(0, left_proj.shape[3])], sem)


def add_kept(kept, s, out):
    out[out.shape[0] - 1] = jnp.full(out.shape[1:], kept[0, 0, s].astype(F32), F32).astype(BF16)


def first_kernel(kept_in, left_proj, out, kept, sems):
    counts = load(kept_in, kept, sems.at[1])
    copy = send_block(0, left_proj, out, sems.at[0])
    counts.wait()
    add_kept(kept, 0, out)
    copy.wait()


def head_kernel(band, kept, boundary, right, row_tensor, left_proj, first, wide, r, left, x, rp, raw, r32, rp32, rpt, h, sems):
    layer = load(row_tensor.at[0, 0], raw, sems.at[0])
    copy = send_block(1, left_proj, left, sems.at[1])
    add_kept(kept, 1, left)

    @pl.when(band[0] == 0)
    def _():
        a = load(right.at[0, 0, 0], rp, sems.at[2])
        b = load(boundary.at[0, 0], x, sems.at[3])
        a.wait()
        flip_right(rp, rp32, rpt)
        b.wait()
        contract_right(x, rpt, h)

    layer.wait()
    spread_layer(raw, r32, r)

    @pl.when(band[0] == 0)
    def _():
        contract_layer(r, h, wide)

    copy.wait()


def wide_kernel(s, n_before, prepares, band, *refs):
    refs = list(refs[n_before:])
    boundary, right, r, wide = (refs.pop(0) for _ in range(4))
    ahead = refs.pop(0) if prepares else None
    rp32, rpt, h = refs

    @pl.when(band[0] == 0)
    def _():
        flip_right(right.at[0, 0, s], rp32, rpt)
        contract_right(boundary.at[0, s], rpt, h)
        contract_layer(r, h, wide, unroll=8)

    if prepares:

        @pl.when(band[0] == 1)
        def _():
            for k in range(right.shape[2]):
                flip_right(right.at[0, 0, k], rp32, ahead.at[k])


def tail_kernel(s, n_out, sends, band, kept, left, wide, *refs):
    refs = list(refs)
    left_proj = refs.pop(0) if sends else None
    outs = [refs.pop(0) for _ in range(n_out)]
    lpt = refs.pop(0)
    send = refs.pop(0) if sends else None
    acc, sems = refs
    if sends:
        copy = send_block(s + 2, left_proj, send, sems.at[0])
        add_kept(kept, s + 2, send)
    flip_left(left, lpt)

    @pl.when(band[0] == 0)
    def _():
        contract_left(lpt, wide, acc, live=live_mask(left, kept[0, 0, s]))
        store(acc, outs)

    if sends:
        copy.wait()


def lower_kernel(s, part, parts, carried, n_before, band, kept, *refs):
    refs = list(refs[n_before:])
    before = refs.pop(0) if carried else None
    arrived, rpt, r, left, lpt, out, h, w, acc = refs
    n = arrived.shape[0]
    last = part == parts - 1

    @pl.when(band[0] == 1)
    def _():
        contract_right(arrived, rpt.at[s], h)
        contract_layer(r, h, w)
        half = lpt.at[:, pl.ds(part * n * h.shape[0], n * h.shape[0])]
        live = live_mask(left, kept[0, 0, s]) if last else None
        contract_left(half, w, acc if last else out, carried=before, live=live)
        if last:
            store(acc, [out])


def end_kernel(s, part, own_places, band, kept, *refs):
    refs = list(refs)
    own = [refs.pop(0) for _ in own_places]
    done = [refs.pop(0) for _ in range(s)]
    before, arrived, rpt, r, left, lpt, out, h, w, acc, block, sems = refs
    n, D, W = arrived.shape

    @pl.when(band[0] == 0)
    def _():
        copies = [
            load(piece, out.at[0, 0, k, pl.ds(at, piece.shape[0])], sems.at[i])
            for i, (piece, (k, at)) in enumerate(zip(own, own_places))
        ]
        for copy in copies:
            copy.wait()

    @pl.when(band[0] == 1)
    def _():
        copies = [load(piece, out.at[0, 0, k], sems.at[k]) for k, piece in enumerate(done)]
        contract_right(arrived, rpt.at[s], h)
        contract_layer(r, h, w)
        half = lpt.at[:, pl.ds(part * n * D, n * D)]
        contract_left(half, w, acc, carried=before, live=live_mask(left, kept[0, 0, s]))
        step = block.shape[0] // 4
        for i in range(4):
            rows = pl.ds(i * step, step)
            block[rows] = acc[i * step * D : (i + 1) * step * D, :].astype(BF16).reshape(step, D, W)
            copies.append(load(block.at[rows], out.at[0, 0, s, rows], sems.at[s + i]))
        for copy in copies:
            copy.wait()


def body(boundary, row_tensor, right_proj, left_proj, kept):
    _, sectors, W, D, _ = boundary.shape
    band = lax.axis_index("band").astype(jnp.int32)[None]
    down = [(0, 1)]
    splits = [2] + [1] * (sectors - 2) + [2]

    block = pltpu.VMEM((W, D, W), BF16)
    ext = pltpu.VMEM((W + 1, D, W), BF16)
    layer = pltpu.VMEM((D * D, D * D), BF16)
    wide_shape = pltpu.VMEM((D, W, D, W), BF16)
    rp32, lpt, acc = pltpu.VMEM((W * D, W), F32), pltpu.VMEM((W, W * D), BF16), pltpu.VMEM((W * D, W), F32)

    def wide_part(n):
        return pltpu.VMEM((D, n, D, W), BF16)

    def cost(part):
        return pl.CostEstimate(
            flops=int(8 * part * W * D * W * W * D), bytes_accessed=8 * W * D * W, transcendentals=0
        )

    def call(kernel, name, part, in_specs, outs, scratch, **kw):
        single = len(outs) == 1
        specs = [ANY if isinstance(o, jax.ShapeDtypeStruct) else VMEM for o in outs]
        return pl.pallas_call(
            kernel, out_shape=outs[0] if single else outs, in_specs=in_specs,
            out_specs=specs[0] if single else specs, scratch_shapes=scratch,
            compiler_params=PARAMS, cost_estimate=cost(part), name=name, **kw,
        )

    rpt = pltpu.VMEM((D // 2, W, 2 * W), BF16)
    dma = pltpu.SemaphoreType.DMA((sectors + 4,))
    direct, (hop, rest) = straight(), around()
    axes = ("col", "band")
    first = call(first_kernel, "first", 0.1, [HBM, HBM], [ext], [pltpu.SMEM(kept.shape, jnp.int32), dma])(
        in_hbm(kept), in_hbm(left_proj)
    )
    left = [in_vmem(lax.ppermute(first, axes, direct))]
    wide, r, send = call(
        head_kernel, "head", 0.75, [SMEM, SMEM] + [HBM] * 4 + [ANY], [wide_shape, layer, ext],
        [block, block, pltpu.VMEM((D, D, D, D), BF16), pltpu.VMEM((D * D * D * D // W, W), F32), rp32, rpt, wide_shape, dma],
    )(band, kept, in_hbm(boundary), in_hbm(right_proj), in_hbm(row_tensor), in_hbm(left_proj), first)
    r, near, right = in_vmem(r), in_vmem(boundary), in_vmem(right_proj)
    states, arrived, flipped = [], [], []

    def tail(s, wide, sends=False):
        k, extra = splits[s], [in_hbm(left_proj)] if sends else []
        outs = call(
            functools.partial(tail_kernel, s, k, sends), "tail", 0.25, [SMEM, SMEM, VMEM, VMEM] + [HBM] * len(extra),
            [pltpu.VMEM((W // k, D, W), BF16)] * k + [lpt] + [ext] * len(extra), [acc, dma],
        )(band, kept, left[s], in_vmem(wide), *extra)
        states.append(list(outs[:k]))
        flipped.append(in_vmem(outs[k]))
        arrived.append([])
        return outs[k + 1 :]

    def give(s, part=0):
        arrived[s].append(lax.ppermute(states[s][part], "band", down))

    def widen(s, before, prepares=False):
        return call(
            functools.partial(wide_kernel, s, len(before), prepares), "wide", 0.75,
            [SMEM] + [ANY] * len(before) + [VMEM] * 3,
            [wide_shape] + ([pltpu.VMEM((sectors, *rpt.shape), BF16)] if prepares else []), [rp32, rpt, wide_shape],
        )(band, *before, near, right, r)

    def lower(s, part, before, total=None):
        k = splits[s]
        carried = [] if total is None else [in_vmem(total)]
        operands = carried + [in_vmem(arrived[s][part]), ahead, r, left[s], flipped[s]]
        return call(
            functools.partial(lower_kernel, s, part, k, bool(carried), len(before)), "lower", 1 / k,
            [SMEM, SMEM] + [ANY] * len(before) + [VMEM] * len(operands), [block if part == k - 1 else acc],
            [wide_part(W // k), wide_part(W // k), acc],
        )(band, kept, *before, *operands)

    left.append(in_vmem(lax.ppermute(send, axes, direct)))
    (send,) = tail(0, wide, True)
    give(0)
    part_way = lax.ppermute(send, axes, hop)
    wide, ahead = widen(1, [states[0][0]], True)
    states[0][1], wide = lax.optimization_barrier((states[0][1], wide))
    give(0, 1)
    ahead = in_vmem(ahead)
    tail(1, wide)
    give(1)
    part_way, states[1][0] = lax.optimization_barrier((part_way, states[1][0]))
    left.append(in_vmem(lax.ppermute(part_way, axes, rest)))
    wide = widen(2, [part_way])
    done = [lower(0, 1, [], lower(0, 0, [wide]))]
    tail(2, wide)
    give(2)
    give(2, 1)
    done.append(lower(1, 0, [states[2][0], done[0]]))
    s, k = sectors - 1, splits[-1]
    total = lower(s, 0, [done[1]])
    own = [x for state in states for x in state]
    places = [(i, W // splits[i] * j) for i in range(sectors) for j in range(splits[i])]
    operands = own + done + [total, arrived[s][k - 1]]
    return call(
        functools.partial(end_kernel, s, k - 1, places), "end", 1 / k, [SMEM, SMEM] + [VMEM] * (len(operands) + 4),
        [jax.ShapeDtypeStruct((1, 1, sectors, W, D, W), BF16)],
        [wide_part(W // k), wide_part(W // k), acc, block, dma],
    )(band, kept, *[in_vmem(x) for x in operands], ahead, r, left[s], flipped[s])


def solution(mesh):
    in_specs = (
        P("col", None, None, None, None),
        P("band", "col", None, None, None, None),
        P("band", "col", None, None, None, None),
        P("band", "col", None, None, None, None),
        P("band", "col", None),
    )
    out_specs = P("band", "col", None, None, None, None)
    return jax.shard_map(body, mesh=mesh, in_specs=in_specs, out_specs=out_specs, check_vma=False)
```

profile of v0, /device:TPU:8, one launch (start us, length us, event | category | flops | bytes accessed | tf_op | source)
XLA Modules:
  0.0 64.8 jit_solution(16758587675061920802)
XLA Ops:
  0.0 0.0 copy-start.2
  0.0 1.1 %first.1 = bf16[129,16,128]{2,1,0:T(8,128)(2,1)S(1)} custom-call(s32[1,1,3]{2,1,0:T(1,128)} %kept.17, bf16[1,1,3,128,16,128]{5,4,3,2,1,0:T(8,128)(2,1)} %refs_0_.1), custom_call_target="tpu_custom_call" | custom-call | flops 429496736 | bytes 2097152 | tf_op jit(solution)/shard_map/first/pallas_call | solution.py:310
  1.1 0.1 collective-permute-start
  1.2 0.0 copy-done.2
  1.2 2.6 %head.1 = (bf16[16,128,16,128]{3,2,1,0:T(8,128)(2,1)S(1)}, bf16[256,256]{1,0:T(8,128)(2,1)S(1)}, bf16[129,16,128]{2,1,0:T(8,128)(2,1)S(1)}) custom-call(s32[1]{0:T(128)} %bitcast.band, s32[1,1,3]{2,1,0:T(1,128)S(1)} %copy-done.2, bf16[1,3,128,16,128]{4,3,2,1,0:T(8,128)(2,1)} %refs_1_.3, bf16[1,1,3,128,16,128]{5,4,3,2,1,0:T(8,128)(2,1)} %refs_2_.3, ...), custom_call_target="tpu_custom_call" | custom-call | flops 3221225472 | bytes 2097152 | tf_op jit(solution)/shard_map/head/pallas_call | solution.py:314
  3.8 2.1 %collective-permute-start.2 = (bf16[129,16,128]{2,1,0:T(8,128)(2,1)S(1)}, bf16[129,16,128]{2,1,0:T(8,128)(2,1)S(1)}, u32[]{:S(2)}, u32[]{:S(2)}) collective-permute-start(bf16[129,16,128]{2,1,0:T(8,128)(2,1)S(1)} %get-tuple-element.30), channel_id=1, source_target_pairs={{254,0},{255,1},{0,2},{1,3},{2,4},{3,5},{4,6},{5,7},{6,8},{7,9},{8... | collective-permute-start | bytes 1585160 | tf_op jit(solution)/shard_map/ppermute | solution.py:352
  5.9 11.4 %collective-permute-done.left.refs_4_ = bf16[129,16,128]{2,1,0:T(8,128)(2,1)S(1)} collective-permute-done((bf16[129,16,128]{2,1,0:T(8,128)(2,1)S(1)}, bf16[129,16,128]{2,1,0:T(8,128)(2,1)S(1)}, u32[]{:S(2)}, u32[]{:S(2)}) %collective-permute-start) | collective-permute-done | bytes 528416 | tf_op jit(solution)/shard_map/ppermute | solution.py:313
  17.3 0.0 copy-start
  17.3 0.0 copy-start.1
  17.3 1.9 %tail.3 = (bf16[64,16,128]{2,1,0:T(8,128)(2,1)S(1)}, bf16[64,16,128]{2,1,0:T(8,128)(2,1)S(1)}, bf16[128,2048]{1,0:T(8,128)(2,1)S(1)}, bf16[129,16,128]{2,1,0:T(8,128)(2,1)S(1)}) custom-call(s32[1]{0:T(128)} %bitcast.band, s32[1,1,3]{2,1,0:T(1,128)S(1)} %copy-done.2, bf16[129,16,128]{2,1,0:T(8,128)(2,1)S(1)} %collective-permute-done.left.refs_4_, ...), custom_call_target="tpu_custom_call" | custom-call | flops 1073741824 | bytes 2097152 | tf_op jit(solution)/shard_map/tail/pallas_call | solution.py:323
  19.3 0.1 collective-permute-start.1
  19.4 1.3 %collective-permute-start.4 = (bf16[64,16,128]{2,1,0:T(8,128)(2,1)S(1)}, bf16[64,16,128]{2,1,0:T(8,128)(2,1)S(1)}, u32[]{:S(2)}, u32[]{:S(2)}) collective-permute-start(bf16[64,16,128]{2,1,0:T(8,128)(2,1)S(1)} %get-tuple-element.24.refs_0_), channel_id=1, source_target_pairs={{0,1},{2,3},{4,5},{6,7},{8,9},{10,11},{12,13},{14,15},{16,17},{18,... | collective-permute-start | bytes 786440 | tf_op jit(solution)/shard_map/ppermute | solution.py:333
  20.7 0.0 copy-done
  20.7 0.0 copy-done.1
  20.7 1.4 %wide.2 = (bf16[16,128,16,128]{3,2,1,0:T(8,128)(2,1)S(1)}, bf16[3,8,128,256]{3,2,1,0:T(8,128)(2,1)S(1)}) custom-call(s32[1]{0:T(128)} %bitcast.band, bf16[64,16,128]{2,1,0:T(8,128)(2,1)S(1)} %get-tuple-element.24.refs_0_, bf16[1,3,128,16,128]{4,3,2,1,0:T(8,128)(2,1)S(1)} %copy-done, bf16[1,1,3,128,16,128]{5,4,3,2,1,0:T(8,128)(2,1)S(1)} %copy-done.1, ...), custom_call_target="tpu_custom_call" | custom-call | flops 3221225472 | bytes 2097152 | tf_op jit(solution)/shard_map/wide/pallas_call | solution.py:336
  22.1 1.3 %collective-permute-start.5 = (bf16[64,16,128]{2,1,0:T(8,128)(2,1)S(1)}, bf16[64,16,128]{2,1,0:T(8,128)(2,1)S(1)}, u32[]{:S(2)}, u32[]{:S(2)}) collective-permute-start(bf16[64,16,128]{2,1,0:T(8,128)(2,1)S(1)} %get-tuple-element.28.refs_1_), channel_id=1, source_target_pairs={{0,1},{2,3},{4,5},{6,7},{8,9},{10,11},{12,13},{14,15},{16,17},{18,... | collective-permute-start | bytes 786440 | tf_op jit(solution)/shard_map/ppermute | solution.py:333
  23.4 0.5 collective-permute-done.2.left.refs_5_
  23.9 0.8 %tail.4 = (bf16[128,16,128]{2,1,0:T(8,128)(2,1)S(1)}, bf16[128,2048]{1,0:T(8,128)(2,1)S(1)}) custom-call(s32[1]{0:T(128)} %bitcast.band, s32[1,1,3]{2,1,0:T(1,128)S(1)} %copy-done.2, bf16[129,16,128]{2,1,0:T(8,128)(2,1)S(1)} %collective-permute-done.2.left.refs_5_, bf16[16,128,16,128]{3,2,1,0:T(8,128)(2,1)S(1)} %get-tuple-element.31.wide), custom_call_target="tpu_custom_call" | custom-call | flops 1073741824 | bytes 2097152 | tf_op jit(solution)/shard_map/tail/pallas_call | solution.py:323
  24.7 1.3 %collective-permute-start.6 = (bf16[128,16,128]{2,1,0:T(8,128)(2,1)S(1)}, bf16[128,16,128]{2,1,0:T(8,128)(2,1)S(1)}, u32[]{:S(2)}, u32[]{:S(2)}) collective-permute-start(bf16[128,16,128]{2,1,0:T(8,128)(2,1)S(1)} %get-tuple-element.33.refs_2_), channel_id=1, source_target_pairs={{0,1},{2,3},{4,5},{6,7},{8,9},{10,11},{12,13},{14,15},{16,17},{18,... | collective-permute-start | bytes 1572872 | tf_op jit(solution)/shard_map/ppermute | solution.py:333
  26.0 4.1 %collective-permute-done.1.refs_0_ = bf16[129,16,128]{2,1,0:T(8,128)(2,1)S(1)} collective-permute-done((bf16[129,16,128]{2,1,0:T(8,128)(2,1)S(1)}, bf16[129,16,128]{2,1,0:T(8,128)(2,1)S(1)}, u32[]{:S(2)}, u32[]{:S(2)}) %collective-permute-start.1) | collective-permute-done | bytes 528416 | tf_op jit(solution)/shard_map/ppermute | solution.py:355
  30.1 5.3 %collective-permute-start.3 = (bf16[129,16,128]{2,1,0:T(8,128)(2,1)S(1)}, bf16[129,16,128]{2,1,0:T(8,128)(2,1)S(1)}, u32[]{:S(2)}, u32[]{:S(2)}) collective-permute-start(bf16[129,16,128]{2,1,0:T(8,128)(2,1)S(1)} %collective-permute-done.1.refs_0_), channel_id=1, source_target_pairs={{2,2},{3,3},{4,4},{5,5},{6,6},{7,7},{8,8},{9,9},{10,10},{11,11},{1... | collective-permute-start | bytes 1585160 | tf_op jit(solution)/shard_map/ppermute | solution.py:363
  35.4 0.0 collective-permute-done.4.refs_1_
  35.4 3.6 %lower.4.refs_0_ = f32[2048,128]{1,0:T(8,128)S(1)} custom-call(s32[1]{0:T(128)} %bitcast.band, s32[1,1,3]{2,1,0:T(1,128)S(1)} %copy-done.2, bf16[16,128,16,128]{3,2,1,0:T(8,128)(2,1)S(1)} %wide.3.refs_0_, bf16[64,16,128]{2,1,0:T(8,128)(2,1)S(1)} %collective-permute-done.4.refs_1_, bf16[3,8,128,256]{3,2,1,0:T(8,128)(2,1)S(1)} %get-tuple-element.37.refs_2_.refs_3_.refs_9_, ...), custom_call_target="tpu_custom_call" | custom-call | flops 2147483648 | bytes 2097152 | tf_op jit(solution)/shard_map/lower/pallas_call | solution.py:346
  39.0 0.0 collective-permute-done.5.refs_1_
  39.0 4.2 %lower.5.refs_1_.refs_5_ = bf16[128,16,128]{2,1,0:T(8,128)(2,1)S(1)} custom-call(s32[1]{0:T(128)} %bitcast.band, s32[1,1,3]{2,1,0:T(1,128)S(1)} %copy-done.2, f32[2048,128]{1,0:T(8,128)S(1)} %lower.4.refs_0_, bf16[64,16,128]{2,1,0:T(8,128)(2,1)S(1)} %collective-permute-done.5.refs_1_, bf16[3,8,128,256]{3,2,1,0:T(8,128)(2,1)S(1)} %get-tuple-element.37.refs_2_.refs_3_.refs_9_, ...), custom_call_target="tpu_custom_call" | custom-call | flops 2147483648 | bytes 2097152 | tf_op jit(solution)/shard_map/lower/pallas_call | solution.py:346
  43.2 0.4 collective-permute-done.3.left.refs_4_.refs_11_
  43.6 0.8 %tail.5 = (bf16[64,16,128]{2,1,0:T(8,128)(2,1)S(1)}, bf16[64,16,128]{2,1,0:T(8,128)(2,1)S(1)}, bf16[128,2048]{1,0:T(8,128)(2,1)S(1)}) custom-call(s32[1]{0:T(128)} %bitcast.band, s32[1,1,3]{2,1,0:T(1,128)S(1)} %copy-done.2, bf16[129,16,128]{2,1,0:T(8,128)(2,1)S(1)} %collective-permute-done.3.left.refs_4_.refs_11_, bf16[16,128,16,128]{3,2,1,0:T(8,128)(2,1)S(1)} %wide.3.refs_0_), custom_call_target="tpu_custom_call" | custom-call | flops 1073741824 | bytes 2097152 | tf_op jit(solution)/shard_map/tail/pallas_call | solution.py:323
  44.4 1.3 %collective-permute-start.7 = (bf16[64,16,128]{2,1,0:T(8,128)(2,1)S(1)}, bf16[64,16,128]{2,1,0:T(8,128)(2,1)S(1)}, u32[]{:S(2)}, u32[]{:S(2)}) collective-permute-start(bf16[64,16,128]{2,1,0:T(8,128)(2,1)S(1)} %get-tuple-element.35.refs_0_.refs_3_), channel_id=1, source_target_pairs={{0,1},{2,3},{4,5},{6,7},{8,9},{10,11},{12,13},{14,15},{16,17},{18,... | collective-permute-start | bytes 786440 | tf_op jit(solution)/shard_map/ppermute | solution.py:333
  45.7 1.3 %collective-permute-start.8 = (bf16[64,16,128]{2,1,0:T(8,128)(2,1)S(1)}, bf16[64,16,128]{2,1,0:T(8,128)(2,1)S(1)}, u32[]{:S(2)}, u32[]{:S(2)}) collective-permute-start(bf16[64,16,128]{2,1,0:T(8,128)(2,1)S(1)} %get-tuple-element.36.refs_4_), channel_id=1, source_target_pairs={{0,1},{2,3},{4,5},{6,7},{8,9},{10,11},{12,13},{14,15},{16,17},{18,... | collective-permute-start | bytes 786440 | tf_op jit(solution)/shard_map/ppermute | solution.py:333
  47.0 0.0 collective-permute-done.6.refs_2_
  47.0 7.0 %lower.6.refs_0_.refs_6_ = bf16[128,16,128]{2,1,0:T(8,128)(2,1)S(1)} custom-call(s32[1]{0:T(128)} %bitcast.band, s32[1,1,3]{2,1,0:T(1,128)S(1)} %copy-done.2, bf16[64,16,128]{2,1,0:T(8,128)(2,1)S(1)} %get-tuple-element.35.refs_0_.refs_3_, bf16[128,16,128]{2,1,0:T(8,128)(2,1)S(1)} %lower.5.refs_1_.refs_5_, ...), custom_call_target="tpu_custom_call" | custom-call | flops 4294967296 | bytes 2097152 | tf_op jit(solution)/shard_map/lower/pallas_call | solution.py:346
  54.1 1.9 %collective-permute-done.7.refs_1_ = bf16[64,16,128]{2,1,0:T(8,128)(2,1)S(1)} collective-permute-done((bf16[64,16,128]{2,1,0:T(8,128)(2,1)S(1)}, bf16[64,16,128]{2,1,0:T(8,128)(2,1)S(1)}, u32[]{:S(2)}, u32[]{:S(2)}) %collective-permute-start.7) | collective-permute-done | bytes 262176 | tf_op jit(solution)/shard_map/ppermute | solution.py:333
  56.0 3.6 %lower.7.refs_7_ = f32[2048,128]{1,0:T(8,128)S(1)} custom-call(s32[1]{0:T(128)} %bitcast.band, s32[1,1,3]{2,1,0:T(1,128)S(1)} %copy-done.2, bf16[128,16,128]{2,1,0:T(8,128)(2,1)S(1)} %lower.6.refs_0_.refs_6_, bf16[64,16,128]{2,1,0:T(8,128)(2,1)S(1)} %collective-permute-done.7.refs_1_, bf16[3,8,128,256]{3,2,1,0:T(8,128)(2,1)S(1)} %get-tuple-element.37.refs_2_.refs_3_.refs_9_, ...), custom_call_target="tpu_custom_call" | custom-call | flops 2147483648 | bytes 2097152 | tf_op jit(solution)/shard_map/lower/pallas_call | solution.py:346
  59.7 0.0 collective-permute-done.8.refs_8_
  59.7 5.0 %end.1 = bf16[1,1,3,128,16,128]{5,4,3,2,1,0:T(8,128)(2,1)} custom-call(s32[1]{0:T(128)} %bitcast.band, s32[1,1,3]{2,1,0:T(1,128)S(1)} %copy-done.2, bf16[64,16,128]{2,1,0:T(8,128)(2,1)S(1)} %get-tuple-element.24.refs_0_, bf16[64,16,128]{2,1,0:T(8,128)(2,1)S(1)} %get-tuple-element.28.refs_1_, bf16[128,16,128]{2,1,0:T(8,128)(2,1)S(1)} %get-tuple-element.33.refs_2_, ...), custom_call_target="tpu_custom_call" | custom-call | flops 2147483648 | bytes 2097152 | tf_op jit(solution)/shard_map/end/pallas_call | solution.py:375
  (1 shorter events, 0.0 us)
Async XLA Ops:
  0.0 1.2 %copy-start.2 = (s32[1,1,3]{2,1,0:T(1,128)S(1)}, s32[1,1,3]{2,1,0:T(1,128)}, u32[]{:S(2)}) copy-start(s32[1,1,3]{2,1,0:T(1,128)} %kept.17) | copy-start | bytes 40
  1.1 16.2 %collective-permute-start = (bf16[129,16,128]{2,1,0:T(8,128)(2,1)S(1)}, bf16[129,16,128]{2,1,0:T(8,128)(2,1)S(1)}, u32[]{:S(2)}, u32[]{:S(2)}) collective-permute-start(bf16[129,16,128]{2,1,0:T(8,128)(2,1)S(1)} %first.1), channel_id=1, source_target_pairs={{254,0},{255,1},{0,2},{1,3},{2,4},{3,5},{4,6},{5,7},{6,8},{7,9},{8... | collective-permute-start | bytes 1585160 | tf_op jit(solution)/shard_map/ppermute | solution.py:313
  3.8 20.1 %collective-permute-start.2 = (bf16[129,16,128]{2,1,0:T(8,128)(2,1)S(1)}, bf16[129,16,128]{2,1,0:T(8,128)(2,1)S(1)}, u32[]{:S(2)}, u32[]{:S(2)}) collective-permute-start(bf16[129,16,128]{2,1,0:T(8,128)(2,1)S(1)} %get-tuple-element.30), channel_id=1, source_target_pairs={{254,0},{255,1},{0,2},{1,3},{2,4},{3,5},{4,6},{5,7},{6,8},{7,9},{8... | collective-permute-start | bytes 1585160 | tf_op jit(solution)/shard_map/ppermute | solution.py:352
  17.3 3.3 %copy-start = (bf16[1,3,128,16,128]{4,3,2,1,0:T(8,128)(2,1)S(1)}, bf16[1,3,128,16,128]{4,3,2,1,0:T(8,128)(2,1)}, u32[]{:S(2)}) copy-start(bf16[1,3,128,16,128]{4,3,2,1,0:T(8,128)(2,1)} %refs_1_.3) | copy-start | bytes 4718596
  17.3 3.3 %copy-start.1 = (bf16[1,1,3,128,16,128]{5,4,3,2,1,0:T(8,128)(2,1)S(1)}, bf16[1,1,3,128,16,128]{5,4,3,2,1,0:T(8,128)(2,1)}, u32[]{:S(2)}) copy-start(bf16[1,1,3,128,16,128]{5,4,3,2,1,0:T(8,128)(2,1)} %refs_2_.3) | copy-start | bytes 4718596
  19.3 10.8 %collective-permute-start.1 = (bf16[129,16,128]{2,1,0:T(8,128)(2,1)S(1)}, bf16[129,16,128]{2,1,0:T(8,128)(2,1)S(1)}, u32[]{:S(2)}, u32[]{:S(2)}) collective-permute-start(bf16[129,16,128]{2,1,0:T(8,128)(2,1)S(1)} %get-tuple-element.29), channel_id=1, source_target_pairs={{0,2},{1,3},{2,4},{3,5},{4,6},{5,7},{6,8},{7,9},{8,10},{9,11},{10,... | collective-permute-start | bytes 1585160 | tf_op jit(solution)/shard_map/ppermute | solution.py:355
  19.4 16.0 %collective-permute-start.4 = (bf16[64,16,128]{2,1,0:T(8,128)(2,1)S(1)}, bf16[64,16,128]{2,1,0:T(8,128)(2,1)S(1)}, u32[]{:S(2)}, u32[]{:S(2)}) collective-permute-start(bf16[64,16,128]{2,1,0:T(8,128)(2,1)S(1)} %get-tuple-element.24.refs_0_), channel_id=1, source_target_pairs={{0,1},{2,3},{4,5},{6,7},{8,9},{10,11},{12,13},{14,15},{16,17},{18,... | collective-permute-start | bytes 786440 | tf_op jit(solution)/shard_map/ppermute | solution.py:333
  22.1 16.9 %collective-permute-start.5 = (bf16[64,16,128]{2,1,0:T(8,128)(2,1)S(1)}, bf16[64,16,128]{2,1,0:T(8,128)(2,1)S(1)}, u32[]{:S(2)}, u32[]{:S(2)}) collective-permute-start(bf16[64,16,128]{2,1,0:T(8,128)(2,1)S(1)} %get-tuple-element.28.refs_1_), channel_id=1, source_target_pairs={{0,1},{2,3},{4,5},{6,7},{8,9},{10,11},{12,13},{14,15},{16,17},{18,... | collective-permute-start | bytes 786440 | tf_op jit(solution)/shard_map/ppermute | solution.py:333
  24.7 22.3 %collective-permute-start.6 = (bf16[128,16,128]{2,1,0:T(8,128)(2,1)S(1)}, bf16[128,16,128]{2,1,0:T(8,128)(2,1)S(1)}, u32[]{:S(2)}, u32[]{:S(2)}) collective-permute-start(bf16[128,16,128]{2,1,0:T(8,128)(2,1)S(1)} %get-tuple-element.33.refs_2_), channel_id=1, source_target_pairs={{0,1},{2,3},{4,5},{6,7},{8,9},{10,11},{12,13},{14,15},{16,17},{18,... | collective-permute-start | bytes 1572872 | tf_op jit(solution)/shard_map/ppermute | solution.py:333
  30.1 13.5 %collective-permute-start.3 = (bf16[129,16,128]{2,1,0:T(8,128)(2,1)S(1)}, bf16[129,16,128]{2,1,0:T(8,128)(2,1)S(1)}, u32[]{:S(2)}, u32[]{:S(2)}) collective-permute-start(bf16[129,16,128]{2,1,0:T(8,128)(2,1)S(1)} %collective-permute-done.1.refs_0_), channel_id=1, source_target_pairs={{2,2},{3,3},{4,4},{5,5},{6,6},{7,7},{8,8},{9,9},{10,10},{11,11},{1... | collective-permute-start | bytes 1585160 | tf_op jit(solution)/shard_map/ppermute | solution.py:363
  44.4 11.6 %collective-permute-start.7 = (bf16[64,16,128]{2,1,0:T(8,128)(2,1)S(1)}, bf16[64,16,128]{2,1,0:T(8,128)(2,1)S(1)}, u32[]{:S(2)}, u32[]{:S(2)}) collective-permute-start(bf16[64,16,128]{2,1,0:T(8,128)(2,1)S(1)} %get-tuple-element.35.refs_0_.refs_3_), channel_id=1, source_target_pairs={{0,1},{2,3},{4,5},{6,7},{8,9},{10,11},{12,13},{14,15},{16,17},{18,... | collective-permute-start | bytes 786440 | tf_op jit(solution)/shard_map/ppermute | solution.py:333
  45.7 13.9 %collective-permute-start.8 = (bf16[64,16,128]{2,1,0:T(8,128)(2,1)S(1)}, bf16[64,16,128]{2,1,0:T(8,128)(2,1)S(1)}, u32[]{:S(2)}, u32[]{:S(2)}) collective-permute-start(bf16[64,16,128]{2,1,0:T(8,128)(2,1)S(1)} %get-tuple-element.36.refs_4_), channel_id=1, source_target_pairs={{0,1},{2,3},{4,5},{6,7},{8,9},{10,11},{12,13},{14,15},{16,17},{18,... | collective-permute-start | bytes 786440 | tf_op jit(solution)/shard_map/ppermute | solution.py:333
where the time goes:
time: 65.1 us; the launch traced here: 64.8 us
  Pallas kernels  32.1 us (49%)
  waiting for transfers between devices  18.4 us (28%)
  starting transfers between devices  14 us (22%)
    pallas_call x4, Pallas kernels, lower(): call(functools.partial(lower_kernel, s, part, k, bool(carried), len(befor...  18.5 us
    ppermute x1, waiting for transfers between devices, body(): left = [in_vmem(lax.ppermute(first, axes, direct))]  11.4 us
    ppermute x5, starting transfers between devices, give(): arrived[s].append(lax.ppermute(states[s][part], 'band', down))  6.46 us
    ppermute x1, starting transfers between devices, body(): left.append(in_vmem(lax.ppermute(part_way, axes, rest)))  5.26 us
    pallas_call x1, Pallas kernels, body(): call(functools.partial(end_kernel, s, k - 1, places), 'end', 1 / k, [SMEM...  4.97 us
    ppermute x1, waiting for transfers between devices, body(): part_way = lax.ppermute(send, axes, hop)  4.09 us
    pallas_call x3, Pallas kernels, tail(): call(functools.partial(tail_kernel, s, k, sends), 'tail', 0.25, [SMEM, SM...  3.5 us
    pallas_call x1, Pallas kernels, body(): call(head_kernel, 'head', 0.75, [SMEM, SMEM] + [HBM] * 4 + [ANY], [wide_s...  2.57 us
  transfers between devices with their start and end apart: 9, of which 5 were waited for; matrix products, arithmetic and copies ran while one was open for 0% of the time, Pallas kernels for 40%

commit v1 on v0

--- a/solution.py
+++ b/solution.py
@@ -159,10 +159,11 @@
     copy.wait()
 
 
-def head_kernel(band, kept, boundary, right, row_tensor, left_proj, first, wide, r, left, x, rp, raw, r32, rp32, rpt, h, sems):
+def head_kernel(band, kept, boundary, right, row_tensor, left_proj, first, wide, r, left, later, x, rp, raw, r32, rp32, rpt, h, sems):
     layer = load(row_tensor.at[0, 0], raw, sems.at[0])
-    copy = send_block(1, left_proj, left, sems.at[1])
+    copies = [send_block(1, left_proj, left, sems.at[1]), send_block(2, left_proj, later, sems.at[4])]
     add_kept(kept, 1, left)
+    add_kept(kept, 2, later)
 
     @pl.when(band[0] == 0)
     def _():
@@ -180,7 +181,8 @@
     def _():
         contract_layer(r, h, wide)
 
-    copy.wait()
+    for copy in copies:
+        copy.wait()
 
 
 def wide_kernel(s, n_before, prepares, band, *refs):
@@ -311,8 +313,8 @@
         in_hbm(kept), in_hbm(left_proj)
     )
     left = [in_vmem(lax.ppermute(first, axes, direct))]
-    wide, r, send = call(
-        head_kernel, "head", 0.75, [SMEM, SMEM] + [HBM] * 4 + [ANY], [wide_shape, layer, ext],
+    wide, r, send, later = call(
+        head_kernel, "head", 0.75, [SMEM, SMEM] + [HBM] * 4 + [ANY], [wide_shape, layer, ext, ext],
         [block, block, pltpu.VMEM((D, D, D, D), BF16), pltpu.VMEM((D * D * D * D // W, W), F32), rp32, rpt, wide_shape, dma],
     )(band, kept, in_hbm(boundary), in_hbm(right_proj), in_hbm(row_tensor), in_hbm(left_proj), first)
     r, near, right = in_vmem(r), in_vmem(boundary), in_vmem(right_proj)
@@ -350,9 +352,10 @@
         )(band, kept, *before, *operands)
 
     left.append(in_vmem(lax.ppermute(send, axes, direct)))
-    (send,) = tail(0, wide, True)
+    tail(0, wide)
+    later, states[0][0] = lax.optimization_barrier((later, states[0][0]))
     give(0)
-    part_way = lax.ppermute(send, axes, hop)
+    part_way = lax.ppermute(later, axes, hop)
     wide, ahead = widen(1, [states[0][0]], True)
     states[0][1], wide = lax.optimization_barrier((states[0][1], wide))
     give(0, 1)

time: 65.1 us -> 64.3 us (0.988)
  Pallas kernels: 32.1 us -> 30.9 us
    pallas_call x3, Pallas kernels: 3.5 us -> 2.38 us  [tail(): call(functools.partial(tail_kernel, s, k, sends), 'tail', 0.25, [SMEM, SM...]
    ppermute x1, waiting for transfers between devices: 0.5 us -> 1.48 us  [body(): left.append(in_vmem(lax.ppermute(send, axes, direct)))]
    ppermute x1, waiting for transfers between devices: 4.09 us -> 3.27 us  [body(): part_way = lax.ppermute(later, axes, hop)]
  transfers between devices with their start and end apart: 9 -> 9, of which waited for: 5 -> 6; matrix products, arithmetic and copies ran while one was open for 0% -> 0% of each run, Pallas kernels for 40% -> 39%
where the time goes in v1:
time: 64.3 us; the launch traced here: 64 us
  Pallas kernels  30.9 us (48%)
  waiting for transfers between devices  18.6 us (29%)
  starting transfers between devices  14.1 us (22%)
    pallas_call x4, Pallas kernels, lower(): call(functools.partial(lower_kernel, s, part, k, bool(carried), len(befor...  18.4 us
    ppermute x1, waiting for transfers between devices, body(): left = [in_vmem(lax.ppermute(first, axes, direct))]  11.4 us
    ppermute x5, starting transfers between devices, give(): arrived[s].append(lax.ppermute(states[s][part], 'band', down))  6.59 us
    ppermute x1, starting transfers between devices, body(): left.append(in_vmem(lax.ppermute(part_way, axes, rest)))  5.29 us
    pallas_call x1, Pallas kernels, body(): call(functools.partial(end_kernel, s, k - 1, places), 'end', 1 / k, [SMEM...  4.97 us
    ppermute x1, waiting for transfers between devices, body(): part_way = lax.ppermute(later, axes, hop)  3.27 us
    pallas_call x1, Pallas kernels, body(): call(head_kernel, 'head', 0.75, [SMEM, SMEM] + [HBM] * 4 + [ANY], [wide_s...  2.57 us
    pallas_call x3, Pallas kernels, tail(): call(functools.partial(tail_kernel, s, k, sends), 'tail', 0.25, [SMEM, SM...  2.38 us
  transfers between devices with their start and end apart: 9, of which 6 were waited for; matrix products, arithmetic and copies ran while one was open for 0% of the time, Pallas kernels for 39%

profile of v1, /device:TPU:8, one launch (start us, length us, event | category | flops | bytes accessed | tf_op | source)
XLA Modules:
  0.0 64.0 jit_solution(12249537737457865967)
XLA Ops:
  0.0 0.0 copy-start.2
  0.0 1.1 %first.1 = bf16[129,16,128]{2,1,0:T(8,128)(2,1)S(1)} custom-call(s32[1,1,3]{2,1,0:T(1,128)} %kept.17, bf16[1,1,3,128,16,128]{5,4,3,2,1,0:T(8,128)(2,1)} %left_proj.3), custom_call_target="tpu_custom_call" | custom-call | flops 429496736 | bytes 2097152 | tf_op jit(solution)/shard_map/first/pallas_call | solution.py:312
  1.1 0.1 collective-permute-start
  1.2 0.0 copy-done.2
  1.2 2.6 %head.1 = (bf16[16,128,16,128]{3,2,1,0:T(8,128)(2,1)S(1)}, bf16[256,256]{1,0:T(8,128)(2,1)S(1)}, bf16[129,16,128]{2,1,0:T(8,128)(2,1)S(1)}, bf16[129,16,128]{2,1,0:T(8,128)(2,1)S(1)}) custom-call(s32[1]{0:T(128)} %bitcast.band, s32[1,1,3]{2,1,0:T(1,128)S(1)} %copy-done.2, bf16[1,3,128,16,128]{4,3,2,1,0:T(8,128)(2,1)} %refs_1_.3, ...), custom_call_target="tpu_custom_call" | custom-call | flops 3221225472 | bytes 2097152 | tf_op jit(solution)/shard_map/head/pallas_call | solution.py:316
  3.8 2.1 %collective-permute-start.2 = (bf16[129,16,128]{2,1,0:T(8,128)(2,1)S(1)}, bf16[129,16,128]{2,1,0:T(8,128)(2,1)S(1)}, u32[]{:S(2)}, u32[]{:S(2)}) collective-permute-start(bf16[129,16,128]{2,1,0:T(8,128)(2,1)S(1)} %get-tuple-element.34), channel_id=1, source_target_pairs={{254,0},{255,1},{0,2},{1,3},{2,4},{3,5},{4,6},{5,7},{6,8},{7,9},{8... | collective-permute-start | bytes 1585160 | tf_op jit(solution)/shard_map/ppermute | solution.py:354
  5.9 11.4 %collective-permute-done.left.refs_4_ = bf16[129,16,128]{2,1,0:T(8,128)(2,1)S(1)} collective-permute-done((bf16[129,16,128]{2,1,0:T(8,128)(2,1)S(1)}, bf16[129,16,128]{2,1,0:T(8,128)(2,1)S(1)}, u32[]{:S(2)}, u32[]{:S(2)}) %collective-permute-start) | collective-permute-done | bytes 528416 | tf_op jit(solution)/shard_map/ppermute | solution.py:315
  17.3 0.0 copy-start
  17.3 0.0 copy-start.1
  17.3 0.8 %tail.3 = (bf16[64,16,128]{2,1,0:T(8,128)(2,1)S(1)}, bf16[64,16,128]{2,1,0:T(8,128)(2,1)S(1)}, bf16[128,2048]{1,0:T(8,128)(2,1)S(1)}) custom-call(s32[1]{0:T(128)} %bitcast.band, s32[1,1,3]{2,1,0:T(1,128)S(1)} %copy-done.2, bf16[129,16,128]{2,1,0:T(8,128)(2,1)S(1)} %collective-permute-done.left.refs_4_, bf16[16,128,16,128]{3,2,1,0:T(8,128)(2,1)S(1)} %get-tuple-element.26.wide), custom_call_target="tpu_custom_call" | custom-call | flops 1073741824 | bytes 2097152 | tf_op jit(solution)/shard_map/tail/pallas_call | solution.py:325
  18.1 0.1 collective-permute-start.1
  18.2 1.4 %collective-permute-start.4 = (bf16[64,16,128]{2,1,0:T(8,128)(2,1)S(1)}, bf16[64,16,128]{2,1,0:T(8,128)(2,1)S(1)}, u32[]{:S(2)}, u32[]{:S(2)}) collective-permute-start(bf16[64,16,128]{2,1,0:T(8,128)(2,1)S(1)} %get-tuple-element.28.refs_0_), channel_id=1, source_target_pairs={{0,1},{2,3},{4,5},{6,7},{8,9},{10,11},{12,13},{14,15},{16,17},{18,... | collective-permute-start | bytes 786440 | tf_op jit(solution)/shard_map/ppermute | solution.py:335
  19.7 0.0 copy-done
  19.7 0.0 copy-done.1
  19.7 1.4 %wide.2 = (bf16[16,128,16,128]{3,2,1,0:T(8,128)(2,1)S(1)}, bf16[3,8,128,256]{3,2,1,0:T(8,128)(2,1)S(1)}) custom-call(s32[1]{0:T(128)} %bitcast.band, bf16[64,16,128]{2,1,0:T(8,128)(2,1)S(1)} %get-tuple-element.28.refs_0_, bf16[1,3,128,16,128]{4,3,2,1,0:T(8,128)(2,1)S(1)} %copy-done, bf16[1,1,3,128,16,128]{5,4,3,2,1,0:T(8,128)(2,1)S(1)} %copy-done.1, ...), custom_call_target="tpu_custom_call" | custom-call | flops 3221225472 | bytes 2097152 | tf_op jit(solution)/shard_map/wide/pallas_call | solution.py:338
  21.1 1.3 %collective-permute-start.5 = (bf16[64,16,128]{2,1,0:T(8,128)(2,1)S(1)}, bf16[64,16,128]{2,1,0:T(8,128)(2,1)S(1)}, u32[]{:S(2)}, u32[]{:S(2)}) collective-permute-start(bf16[64,16,128]{2,1,0:T(8,128)(2,1)S(1)} %get-tuple-element.32.refs_1_), channel_id=1, source_target_pairs={{0,1},{2,3},{4,5},{6,7},{8,9},{10,11},{12,13},{14,15},{16,17},{18,... | collective-permute-start | bytes 786440 | tf_op jit(solution)/shard_map/ppermute | solution.py:335
  22.4 1.5 %collective-permute-done.2.left.refs_5_ = bf16[129,16,128]{2,1,0:T(8,128)(2,1)S(1)} collective-permute-done((bf16[129,16,128]{2,1,0:T(8,128)(2,1)S(1)}, bf16[129,16,128]{2,1,0:T(8,128)(2,1)S(1)}, u32[]{:S(2)}, u32[]{:S(2)}) %collective-permute-start.2) | collective-permute-done | bytes 528416 | tf_op jit(solution)/shard_map/ppermute | solution.py:354
  23.9 0.8 %tail.4 = (bf16[128,16,128]{2,1,0:T(8,128)(2,1)S(1)}, bf16[128,2048]{1,0:T(8,128)(2,1)S(1)}) custom-call(s32[1]{0:T(128)} %bitcast.band, s32[1,1,3]{2,1,0:T(1,128)S(1)} %copy-done.2, bf16[129,16,128]{2,1,0:T(8,128)(2,1)S(1)} %collective-permute-done.2.left.refs_5_, bf16[16,128,16,128]{3,2,1,0:T(8,128)(2,1)S(1)} %get-tuple-element.35.wide), custom_call_target="tpu_custom_call" | custom-call | flops 1073741824 | bytes 2097152 | tf_op jit(solution)/shard_map/tail/pallas_call | solution.py:325
  24.7 1.3 %collective-permute-start.6 = (bf16[128,16,128]{2,1,0:T(8,128)(2,1)S(1)}, bf16[128,16,128]{2,1,0:T(8,128)(2,1)S(1)}, u32[]{:S(2)}, u32[]{:S(2)}) collective-permute-start(bf16[128,16,128]{2,1,0:T(8,128)(2,1)S(1)} %get-tuple-element.37.refs_2_), channel_id=1, source_target_pairs={{0,1},{2,3},{4,5},{6,7},{8,9},{10,11},{12,13},{14,15},{16,17},{18,... | collective-permute-start | bytes 1572872 | tf_op jit(solution)/shard_map/ppermute | solution.py:335
  26.0 3.3 %collective-permute-done.1.refs_0_ = bf16[129,16,128]{2,1,0:T(8,128)(2,1)S(1)} collective-permute-done((bf16[129,16,128]{2,1,0:T(8,128)(2,1)S(1)}, bf16[129,16,128]{2,1,0:T(8,128)(2,1)S(1)}, u32[]{:S(2)}, u32[]{:S(2)}) %collective-permute-start.1) | collective-permute-done | bytes 528416 | tf_op jit(solution)/shard_map/ppermute | solution.py:358
  29.3 5.3 %collective-permute-start.3 = (bf16[129,16,128]{2,1,0:T(8,128)(2,1)S(1)}, bf16[129,16,128]{2,1,0:T(8,128)(2,1)S(1)}, u32[]{:S(2)}, u32[]{:S(2)}) collective-permute-start(bf16[129,16,128]{2,1,0:T(8,128)(2,1)S(1)} %collective-permute-done.1.refs_0_), channel_id=1, source_target_pairs={{2,2},{3,3},{4,4},{5,5},{6,6},{7,7},{8,8},{9,9},{10,10},{11,11},{1... | collective-permute-start | bytes 1585160 | tf_op jit(solution)/shard_map/ppermute | solution.py:366
  34.6 0.0 collective-permute-done.4.refs_1_
  34.6 3.6 %lower.4.refs_0_ = f32[2048,128]{1,0:T(8,128)S(1)} custom-call(s32[1]{0:T(128)} %bitcast.band, s32[1,1,3]{2,1,0:T(1,128)S(1)} %copy-done.2, bf16[16,128,16,128]{3,2,1,0:T(8,128)(2,1)S(1)} %wide.3.refs_0_, bf16[64,16,128]{2,1,0:T(8,128)(2,1)S(1)} %collective-permute-done.4.refs_1_, bf16[3,8,128,256]{3,2,1,0:T(8,128)(2,1)S(1)} %get-tuple-element.41.refs_2_.refs_3_.refs_9_, ...), custom_call_target="tpu_custom_call" | custom-call | flops 2147483648 | bytes 2097152 | tf_op jit(solution)/shard_map/lower/pallas_call | solution.py:348
  38.2 0.0 collective-permute-done.5.refs_1_
  38.3 4.2 %lower.5.refs_1_.refs_5_ = bf16[128,16,128]{2,1,0:T(8,128)(2,1)S(1)} custom-call(s32[1]{0:T(128)} %bitcast.band, s32[1,1,3]{2,1,0:T(1,128)S(1)} %copy-done.2, f32[2048,128]{1,0:T(8,128)S(1)} %lower.4.refs_0_, bf16[64,16,128]{2,1,0:T(8,128)(2,1)S(1)} %collective-permute-done.5.refs_1_, bf16[3,8,128,256]{3,2,1,0:T(8,128)(2,1)S(1)} %get-tuple-element.41.refs_2_.refs_3_.refs_9_, ...), custom_call_target="tpu_custom_call" | custom-call | flops 2147483648 | bytes 2097152 | tf_op jit(solution)/shard_map/lower/pallas_call | solution.py:348
  42.4 0.2 collective-permute-done.3.left.refs_4_.refs_11_
  42.6 0.8 %tail.5 = (bf16[64,16,128]{2,1,0:T(8,128)(2,1)S(1)}, bf16[64,16,128]{2,1,0:T(8,128)(2,1)S(1)}, bf16[128,2048]{1,0:T(8,128)(2,1)S(1)}) custom-call(s32[1]{0:T(128)} %bitcast.band, s32[1,1,3]{2,1,0:T(1,128)S(1)} %copy-done.2, bf16[129,16,128]{2,1,0:T(8,128)(2,1)S(1)} %collective-permute-done.3.left.refs_4_.refs_11_, bf16[16,128,16,128]{3,2,1,0:T(8,128)(2,1)S(1)} %wide.3.refs_0_), custom_call_target="tpu_custom_call" | custom-call | flops 1073741824 | bytes 2097152 | tf_op jit(solution)/shard_map/tail/pallas_call | solution.py:325
  43.4 1.3 %collective-permute-start.7 = (bf16[64,16,128]{2,1,0:T(8,128)(2,1)S(1)}, bf16[64,16,128]{2,1,0:T(8,128)(2,1)S(1)}, u32[]{:S(2)}, u32[]{:S(2)}) collective-permute-start(bf16[64,16,128]{2,1,0:T(8,128)(2,1)S(1)} %get-tuple-element.39.refs_0_.refs_3_), channel_id=1, source_target_pairs={{0,1},{2,3},{4,5},{6,7},{8,9},{10,11},{12,13},{14,15},{16,17},{18,... | collective-permute-start | bytes 786440 | tf_op jit(solution)/shard_map/ppermute | solution.py:335
  44.7 1.3 %collective-permute-start.8 = (bf16[64,16,128]{2,1,0:T(8,128)(2,1)S(1)}, bf16[64,16,128]{2,1,0:T(8,128)(2,1)S(1)}, u32[]{:S(2)}, u32[]{:S(2)}) collective-permute-start(bf16[64,16,128]{2,1,0:T(8,128)(2,1)S(1)} %get-tuple-element.40.refs_4_), channel_id=1, source_target_pairs={{0,1},{2,3},{4,5},{6,7},{8,9},{10,11},{12,13},{14,15},{16,17},{18,... | collective-permute-start | bytes 786440 | tf_op jit(solution)/shard_map/ppermute | solution.py:335
  46.0 0.7 %collective-permute-done.6.refs_2_ = bf16[128,16,128]{2,1,0:T(8,128)(2,1)S(1)} collective-permute-done((bf16[128,16,128]{2,1,0:T(8,128)(2,1)S(1)}, bf16[128,16,128]{2,1,0:T(8,128)(2,1)S(1)}, u32[]{:S(2)}, u32[]{:S(2)}) %collective-permute-start.6) | collective-permute-done | bytes 524320 | tf_op jit(solution)/shard_map/ppermute | solution.py:335
  46.8 7.0 %lower.6.refs_0_.refs_6_ = bf16[128,16,128]{2,1,0:T(8,128)(2,1)S(1)} custom-call(s32[1]{0:T(128)} %bitcast.band, s32[1,1,3]{2,1,0:T(1,128)S(1)} %copy-done.2, bf16[64,16,128]{2,1,0:T(8,128)(2,1)S(1)} %get-tuple-element.39.refs_0_.refs_3_, bf16[128,16,128]{2,1,0:T(8,128)(2,1)S(1)} %lower.5.refs_1_.refs_5_, ...), custom_call_target="tpu_custom_call" | custom-call | flops 4294967296 | bytes 2097152 | tf_op jit(solution)/shard_map/lower/pallas_call | solution.py:348
  53.8 1.4 %collective-permute-done.7.refs_1_ = bf16[64,16,128]{2,1,0:T(8,128)(2,1)S(1)} collective-permute-done((bf16[64,16,128]{2,1,0:T(8,128)(2,1)S(1)}, bf16[64,16,128]{2,1,0:T(8,128)(2,1)S(1)}, u32[]{:S(2)}, u32[]{:S(2)}) %collective-permute-start.7) | collective-permute-done | bytes 262176 | tf_op jit(solution)/shard_map/ppermute | solution.py:335
  55.2 3.6 %lower.7.refs_7_ = f32[2048,128]{1,0:T(8,128)S(1)} custom-call(s32[1]{0:T(128)} %bitcast.band, s32[1,1,3]{2,1,0:T(1,128)S(1)} %copy-done.2, bf16[128,16,128]{2,1,0:T(8,128)(2,1)S(1)} %lower.6.refs_0_.refs_6_, bf16[64,16,128]{2,1,0:T(8,128)(2,1)S(1)} %collective-permute-done.7.refs_1_, bf16[3,8,128,256]{3,2,1,0:T(8,128)(2,1)S(1)} %get-tuple-element.41.refs_2_.refs_3_.refs_9_, ...), custom_call_target="tpu_custom_call" | custom-call | flops 2147483648 | bytes 2097152 | tf_op jit(solution)/shard_map/lower/pallas_call | solution.py:348
  58.9 0.0 collective-permute-done.8.refs_8_
  58.9 5.0 %end.1 = bf16[1,1,3,128,16,128]{5,4,3,2,1,0:T(8,128)(2,1)} custom-call(s32[1]{0:T(128)} %bitcast.band, s32[1,1,3]{2,1,0:T(1,128)S(1)} %copy-done.2, bf16[64,16,128]{2,1,0:T(8,128)(2,1)S(1)} %get-tuple-element.28.refs_0_, bf16[64,16,128]{2,1,0:T(8,128)(2,1)S(1)} %get-tuple-element.32.refs_1_, bf16[128,16,128]{2,1,0:T(8,128)(2,1)S(1)} %get-tuple-element.37.refs_2_, ...), custom_call_target="tpu_custom_call" | custom-call | flops 2147483648 | bytes 2097152 | tf_op jit(solution)/shard_map/end/pallas_call | solution.py:378
  (1 shorter events, 0.0 us)
Async XLA Ops:
  0.0 1.2 %copy-start.2 = (s32[1,1,3]{2,1,0:T(1,128)S(1)}, s32[1,1,3]{2,1,0:T(1,128)}, u32[]{:S(2)}) copy-start(s32[1,1,3]{2,1,0:T(1,128)} %kept.17) | copy-start | bytes 40
  1.1 16.2 %collective-permute-start = (bf16[129,16,128]{2,1,0:T(8,128)(2,1)S(1)}, bf16[129,16,128]{2,1,0:T(8,128)(2,1)S(1)}, u32[]{:S(2)}, u32[]{:S(2)}) collective-permute-start(bf16[129,16,128]{2,1,0:T(8,128)(2,1)S(1)} %first.1), channel_id=1, source_target_pairs={{254,0},{255,1},{0,2},{1,3},{2,4},{3,5},{4,6},{5,7},{6,8},{7,9},{8... | collective-permute-start | bytes 1585160 | tf_op jit(solution)/shard_map/ppermute | solution.py:315
  3.8 20.1 %collective-permute-start.2 = (bf16[129,16,128]{2,1,0:T(8,128)(2,1)S(1)}, bf16[129,16,128]{2,1,0:T(8,128)(2,1)S(1)}, u32[]{:S(2)}, u32[]{:S(2)}) collective-permute-start(bf16[129,16,128]{2,1,0:T(8,128)(2,1)S(1)} %get-tuple-element.34), channel_id=1, source_target_pairs={{254,0},{255,1},{0,2},{1,3},{2,4},{3,5},{4,6},{5,7},{6,8},{7,9},{8... | collective-permute-start | bytes 1585160 | tf_op jit(solution)/shard_map/ppermute | solution.py:354
  17.3 2.3 %copy-start = (bf16[1,3,128,16,128]{4,3,2,1,0:T(8,128)(2,1)S(1)}, bf16[1,3,128,16,128]{4,3,2,1,0:T(8,128)(2,1)}, u32[]{:S(2)}) copy-start(bf16[1,3,128,16,128]{4,3,2,1,0:T(8,128)(2,1)} %refs_1_.3) | copy-start | bytes 4718596
  17.3 2.3 %copy-start.1 = (bf16[1,1,3,128,16,128]{5,4,3,2,1,0:T(8,128)(2,1)S(1)}, bf16[1,1,3,128,16,128]{5,4,3,2,1,0:T(8,128)(2,1)}, u32[]{:S(2)}) copy-start(bf16[1,1,3,128,16,128]{5,4,3,2,1,0:T(8,128)(2,1)} %refs_2_.3) | copy-start | bytes 4718596
  18.1 11.1 %collective-permute-start.1 = (bf16[129,16,128]{2,1,0:T(8,128)(2,1)S(1)}, bf16[129,16,128]{2,1,0:T(8,128)(2,1)S(1)}, u32[]{:S(2)}, u32[]{:S(2)}) collective-permute-start(bf16[129,16,128]{2,1,0:T(8,128)(2,1)S(1)} %get-tuple-element.33), channel_id=1, source_target_pairs={{0,2},{1,3},{2,4},{3,5},{4,6},{5,7},{6,8},{7,9},{8,10},{9,11},{10,... | collective-permute-start | bytes 1585160 | tf_op jit(solution)/shard_map/ppermute | solution.py:358
  18.2 16.4 %collective-permute-start.4 = (bf16[64,16,128]{2,1,0:T(8,128)(2,1)S(1)}, bf16[64,16,128]{2,1,0:T(8,128)(2,1)S(1)}, u32[]{:S(2)}, u32[]{:S(2)}) collective-permute-start(bf16[64,16,128]{2,1,0:T(8,128)(2,1)S(1)} %get-tuple-element.28.refs_0_), channel_id=1, source_target_pairs={{0,1},{2,3},{4,5},{6,7},{8,9},{10,11},{12,13},{14,15},{16,17},{18,... | collective-permute-start | bytes 786440 | tf_op jit(solution)/shard_map/ppermute | solution.py:335
  21.1 17.1 %collective-permute-start.5 = (bf16[64,16,128]{2,1,0:T(8,128)(2,1)S(1)}, bf16[64,16,128]{2,1,0:T(8,128)(2,1)S(1)}, u32[]{:S(2)}, u32[]{:S(2)}) collective-permute-start(bf16[64,16,128]{2,1,0:T(8,128)(2,1)S(1)} %get-tuple-element.32.refs_1_), channel_id=1, source_target_pairs={{0,1},{2,3},{4,5},{6,7},{8,9},{10,11},{12,13},{14,15},{16,17},{18,... | collective-permute-start | bytes 786440 | tf_op jit(solution)/shard_map/ppermute | solution.py:335
  24.7 22.1 %collective-permute-start.6 = (bf16[128,16,128]{2,1,0:T(8,128)(2,1)S(1)}, bf16[128,16,128]{2,1,0:T(8,128)(2,1)S(1)}, u32[]{:S(2)}, u32[]{:S(2)}) collective-permute-start(bf16[128,16,128]{2,1,0:T(8,128)(2,1)S(1)} %get-tuple-element.37.refs_2_), channel_id=1, source_target_pairs={{0,1},{2,3},{4,5},{6,7},{8,9},{10,11},{12,13},{14,15},{16,17},{18,... | collective-permute-start | bytes 1572872 | tf_op jit(solution)/shard_map/ppermute | solution.py:335
  29.3 13.4 %collective-permute-start.3 = (bf16[129,16,128]{2,1,0:T(8,128)(2,1)S(1)}, bf16[129,16,128]{2,1,0:T(8,128)(2,1)S(1)}, u32[]{:S(2)}, u32[]{:S(2)}) collective-permute-start(bf16[129,16,128]{2,1,0:T(8,128)(2,1)S(1)} %collective-permute-done.1.refs_0_), channel_id=1, source_target_pairs={{2,2},{3,3},{4,4},{5,5},{6,6},{7,7},{8,8},{9,9},{10,10},{11,11},{1... | collective-permute-start | bytes 1585160 | tf_op jit(solution)/shard_map/ppermute | solution.py:366
  43.4 11.8 %collective-permute-start.7 = (bf16[64,16,128]{2,1,0:T(8,128)(2,1)S(1)}, bf16[64,16,128]{2,1,0:T(8,128)(2,1)S(1)}, u32[]{:S(2)}, u32[]{:S(2)}) collective-permute-start(bf16[64,16,128]{2,1,0:T(8,128)(2,1)S(1)} %get-tuple-element.39.refs_0_.refs_3_), channel_id=1, source_target_pairs={{0,1},{2,3},{4,5},{6,7},{8,9},{10,11},{12,13},{14,15},{16,17},{18,... | collective-permute-start | bytes 786440 | tf_op jit(solution)/shard_map/ppermute | solution.py:335
  44.7 14.1 %collective-permute-start.8 = (bf16[64,16,128]{2,1,0:T(8,128)(2,1)S(1)}, bf16[64,16,128]{2,1,0:T(8,128)(2,1)S(1)}, u32[]{:S(2)}, u32[]{:S(2)}) collective-permute-start(bf16[64,16,128]{2,1,0:T(8,128)(2,1)S(1)} %get-tuple-element.40.refs_4_), channel_id=1, source_target_pairs={{0,1},{2,3},{4,5},{6,7},{8,9},{10,11},{12,13},{14,15},{16,17},{18,... | collective-permute-start | bytes 786440 | tf_op jit(solution)/shard_map/ppermute | solution.py:335
